TPU v7x, 32 devices: a whole 2x2x4 slice. The times are simulated.
32 devices in a mesh: ga: 2 (over y), gx: 4 (over z), gy: 2 (over x), gz: 2 (over core).
Axes of the slice: x: 2, y: 2, z: 4, core: 2. Of those that a mesh axis runs over, the one named last changes fastest.
Arguments:
- state: bfloat16 [8, 256, 4, 512], P(('ga', 'gx'), None, None, 'gy'), parts along dimension 0, may hold values from -6 to 6
- left_env: bfloat16 [16, 8, 256, 256], P(None, ('ga', 'gx')), parts along dimension 1, may hold values from -0.375 to 0.375
- mpo_terms: bfloat16 [16, 16, 4, 4], P(None, 'gz'), may hold values from -0.75 to 0.75
- right_env: bfloat16 [16, 1024, 256], P('gz', ('ga', 'gy')), parts along dimension 1, may hold values from -0.09375 to 0.09375
- term_charge: int32 [16], replicated, may hold values from 0 to 2, as said below
- charge_order: int32 [8], P('ga'), parts along dimension 0, may hold values from 0 to 3, as said below
- sector_dims: int32 [8], P('ga'), parts along dimension 0, may hold values from 128 to 256
Outputs:
- result_state: bfloat16 [8, 256, 4, 512], P(('ga', 'gx'), None, 'gz', 'gy'), parts along dimension 0
There are 2 independent parts, one for each index of `ga`. A program takes and returns all parts, laid end to end along the dimension named above; an argument that names none is the same for every part. Nothing has to cross between parts.
Inputs may be any that keep to these rules, and one draw needn't show every extreme that they name: `charge_order`: each value appears once. `term_charge`: each of 0, 1 and 2 appears at least once.
All inputs are finite; a program needn't handle non-finite values.
Results may differ from a plain program's by a relative error of at most 0.0057.
Values may be sent and summed in bfloat16 or wider, within the bound.
No kernel may reach another device: no remote copies, remote signals or barrier semaphores. Data moves between devices by JAX's collectives and lax.ppermute only.
A program may use at most 64 MiB of HBM per device.

v0:
```python
import jax
import jax.numpy as jnp
from jax import lax
from jax.experimental import pallas as pl
from jax.experimental.pallas import tpu as pltpu
from jax.sharding import PartitionSpec as P


LANE_ROWS = 16
BF16 = jnp.bfloat16
F32 = jnp.float32
VMEM_SPEC = pl.BlockSpec(memory_space=pltpu.VMEM)
SMEM_SPEC = pl.BlockSpec(memory_space=pltpu.SMEM)


def dot(a, b):
    return jnp.dot(a, b, preferred_element_type=F32)


def iota(shape, axis):
    return lax.broadcasted_iota(jnp.int32, shape, axis)


def mix_right(mpo_rows, right_own, right_other, terms, phys, phys_own):
    share, rows, cols = right_own.shape
    right_count = 2 * share
    depth = right_count * LANE_ROWS
    tiles = 2
    groups = terms * phys
    lhs_rows = groups * phys_own * LANE_ROWS
    chunk = LANE_ROWS * phys_own * phys * 2

    def kernel(mpo_ref, own_ref, other_ref, out_ref, lhs):
        core = lax.axis_index("gz")

        @pl.when(pl.program_id(0) == 0)
        def _():
            row = iota((lhs_rows, groups * phys), 0) // LANE_ROWS
            wanted = (row // phys_own) * phys + core * phys_own + row % phys_own
            spread = (iota((lhs_rows, groups * phys), 1) == wanted).astype(F32).astype(BF16)
            tall = dot(spread, mpo_ref[...]).astype(BF16)
            widen = (iota((right_count, depth), 1) // LANE_ROWS == iota((right_count, depth), 0))
            wide = dot(tall, widen.astype(F32).astype(BF16))
            same = iota(wide.shape, 0) % LANE_ROWS == iota(wide.shape, 1) % LANE_ROWS
            lhs[...] = jnp.where(same, wide, 0.0).astype(BF16)

        for t in range(tiles):
            tile = pl.ds(t * LANE_ROWS, LANE_ROWS)
            rhs = jnp.concatenate(
                [
                    own_ref[:, tile, :].reshape(share * LANE_ROWS, cols),
                    other_ref[:, tile, :].reshape(share * LANE_ROWS, cols),
                ],
                0,
            )
            for start in range(0, lhs_rows, chunk):
                part = dot(lhs[start : start + chunk, :], rhs).astype(BF16)
                part = part.reshape(chunk // LANE_ROWS, LANE_ROWS, cols)
                for i in range(chunk // LANE_ROWS):
                    group, p = divmod(start // LANE_ROWS + i, phys_own)
                    out_ref[group, t, :, p * cols : (p + 1) * cols] = part[i]

    row_tiles = rows // LANE_ROWS
    out = pl.pallas_call(
        kernel,
        out_shape=jax.ShapeDtypeStruct((groups, row_tiles, LANE_ROWS, phys_own * cols), BF16),
        grid=(row_tiles // tiles,),
        in_specs=[
            pl.BlockSpec(mpo_rows.shape, lambda t: (0, 0)),
            pl.BlockSpec((share, tiles * LANE_ROWS, cols), lambda t: (0, t, 0)),
            pl.BlockSpec((share, tiles * LANE_ROWS, cols), lambda t: (0, t, 0)),
        ],
        out_specs=pl.BlockSpec(
            (groups, tiles, LANE_ROWS, phys_own * cols), lambda t: (0, t, 0, 0)
        ),
        scratch_shapes=[pltpu.VMEM((lhs_rows, depth), BF16)],
        compiler_params=pltpu.CompilerParams(
            dimension_semantics=("arbitrary",), vmem_limit_bytes=16 << 20
        ),
        cost_estimate=pl.CostEstimate(
            flops=2 * lhs_rows * depth * cols * row_tiles,
            bytes_accessed=2 * groups * rows * phys_own * cols,
            transcendentals=0,
        ),
        name="mix_right",
    )(mpo_rows, right_own, right_other)
    return out.reshape(terms, phys * rows, phys_own * cols)


def apply_block(hop, partner, parts, total, left, mixed, charges, order, dims=None):
    terms = left.shape[0]
    out_cols = mixed.shape[2]
    depth = left.shape[2]
    rows = left.shape[1]
    blocks = [block for block, _ in parts]
    flags = [swapped for _, swapped in parts]
    half, _, cols = blocks[0].shape
    first = total is None

    def kernel(charges_ref, order_ref, *refs):
        refs = list(refs)
        dims_ref = refs.pop(0) if dims is not None else None
        total_ref = refs.pop(0) if not first else None
        left_ref, mixed_ref = refs[0], refs[1]
        block_refs = refs[2 : 2 + len(blocks)]
        out_ref = refs[2 + len(blocks)]
        acc = refs[3 + len(blocks)] if dims is not None else out_ref
        me, core = lax.axis_index("gx"), lax.axis_index("gz")
        shift = order_ref[partner(me, hop)] - order_ref[me] + 1
        acc[...] = jnp.zeros_like(acc) if first else total_ref[...]

        def term(u, carry):
            @pl.when(charges_ref[u] == shift)
            def _():
                env = left_ref[u]
                sums = None
                for ref, swapped in zip(block_refs, flags):
                    which = 1 - core if swapped else core
                    source = jnp.concatenate([ref[q] for q in range(half)], 1)
                    applied = dot(env, source).astype(BF16)
                    begin = pl.multiple_of(which * (half * cols), half * cols)
                    piece = dot(applied, mixed_ref[u, pl.ds(begin, half * cols), :])
                    sums = piece if sums is None else sums + piece
                acc[...] += sums

            return carry

        lax.fori_loop(0, terms, term, 0)
        if dims is not None:
            keep = iota((rows, out_cols), 0) < dims_ref[me]
            masked = jnp.where(keep, acc[...], 0.0).astype(BF16)
            count = out_cols // cols
            for p in range(count):
                out_ref[p] = masked[:, p * cols : (p + 1) * cols]

    scratch = [] if dims is None else [pltpu.VMEM((rows, out_cols), F32)]
    if dims is None:
        out_shape = jax.ShapeDtypeStruct((rows, out_cols), F32)
    else:
        out_shape = jax.ShapeDtypeStruct((out_cols // cols, rows, cols), BF16)
    scalars = [charges, order] + ([] if dims is None else [dims])
    arrays = ([] if first else [total]) + [left, mixed] + blocks
    return pl.pallas_call(
        kernel,
        out_shape=out_shape,
        in_specs=[SMEM_SPEC] * len(scalars) + [VMEM_SPEC] * len(arrays),
        out_specs=VMEM_SPEC,
        scratch_shapes=scratch,
        compiler_params=pltpu.CompilerParams(vmem_limit_bytes=8 << 20),
        cost_estimate=pl.CostEstimate(
            flops=2 * (terms // 3) * rows * half * cols * len(blocks) * (depth + out_cols),
            bytes_accessed=2 * rows * out_cols * 4,
            transcendentals=0,
        ),
        name="apply_block",
    )(*scalars, *arrays)


def gather_blocks(own, axis):
    count = lax.axis_size(axis)
    if count & (count - 1):
        blocks = {}
        for hop in range(1, count):
            pairs = [(i, (i + hop) % count) for i in range(count)]
            blocks[hop] = lax.ppermute(own, axis, pairs)
        return blocks, lambda me, hop: lax.rem(me - hop + count, count)
    blocks = {0: own}
    bit = count // 2
    while bit:
        pairs = [(i, i ^ bit) for i in range(count)]
        for hop in list(blocks):
            blocks[hop | bit] = lax.ppermute(blocks[hop], axis, pairs)
        bit //= 2
    del blocks[0]
    return blocks, lambda me, hop: lax.bitwise_xor(me, hop)


def use_order(count):
    return sorted(range(1, count), key=lambda hop: (bin(hop).count("1"), -hop))


def step(state, left_env, mpo_terms, right_env, term_charge, charge_order, sector_dims):
    terms, share, phys, _ = mpo_terms.shape
    cores = lax.axis_size("gz")
    assert state.shape[0] == 1 and cores == 2
    half = phys // cores
    core = lax.axis_index("gz")
    swap = [(0, 1), (1, 0)]
    planes = state[0].transpose(1, 0, 2)
    own = lax.dynamic_slice_in_dim(planes, core * half, half, 0)
    blocks, partner = gather_blocks(own, "gx")
    right_other = lax.ppermute(right_env, "gz", swap)
    mpo_other = lax.ppermute(mpo_terms, "gz", swap)
    mpo_all = jnp.concatenate([mpo_terms, mpo_other], 1)
    mpo_rows = mpo_all.transpose(0, 3, 2, 1).reshape(terms * phys * phys, cores * share)
    mixed = mix_right(mpo_rows, right_env, right_other, terms, phys, half)
    left = left_env[:, 0]

    own_other = lax.dynamic_slice_in_dim(planes, (1 - core) * half, half, 0)
    own_parts = [(own, False), (own_other, True)]
    total = apply_block(
        0, partner, own_parts, None, left, mixed, term_charge, charge_order
    )
    hops = use_order(lax.axis_size("gx"))
    for hop in hops:
        other = lax.ppermute(blocks[hop], "gz", swap)
        dims = sector_dims if hop == hops[-1] else None
        parts = [(blocks[hop], False), (other, True)]
        total = apply_block(
            hop, partner, parts, total, left, mixed, term_charge, charge_order, dims
        )
    return total.transpose(1, 0, 2)[None]


def solution(mesh):
    return jax.shard_map(
        step,
        mesh=mesh,
        in_specs=(
            P(("ga", "gx"), None, None, "gy"),
            P(None, ("ga", "gx"), None, None),
            P(None, "gz", None, None),
            P("gz", ("ga", "gy"), None),
            P(),
            P("ga"),
            P("ga"),
        ),
        out_specs=P(("ga", "gx"), None, "gz", "gy"),
        check_vma=False,
    )
```

profile of v0, /device:TPU:0, one launch (start us, length us, event | category | flops | bytes accessed | tf_op | source)
XLA Modules:
  0.0 51.4 jit_solution(5763377617100087325)
XLA Ops:
  0.0 0.6 %collective-permute-start.1 = (bf16[8,256,256]{2,1,0:T(8,128)(2,1)}, bf16[8,256,256]{2,1,0:T(8,128)(2,1)}, u32[]{:S(2)}, u32[]{:S(2)}) collective-permute-start(bf16[8,256,256]{2,1,0:T(8,128)(2,1)} %own_ref.1), channel_id=1, source_target_pairs={{0,1},{1,0},{2,3},{3,2},{4,5},{5,4},{6,7},{7,6},{8,9},{9,8},{10,11... | collective-permute-start | bytes 3145736 | tf_op jit(solution)/shard_map/ppermute | solution.py:192
  0.6 1.8 %constant_dynamic-slice_fusion = (bf16[1,256,2,256]{3,2,1,0:T(2,128)(2,1)S(1)}, bf16[1,256,2,256]{3,2,1,0:T(2,128)(2,1)S(1)}) fusion(bf16[1,256,4,256]{3,2,1,0:T(4,128)(2,1)} %param.7, s32[]{:T(128)S(6)} %select_n.7, s32[]{:T(128)S(6)} %select_n.6), kind=kLoop, calls=%fused_computation.3 | loop fusion | bytes 1048584 | tf_op jit(solution)/shard_map/dynamic-slice.3
  2.4 3.7 %collective-permute-start.2 = (bf16[2,256,256]{2,1,0:T(8,128)(2,1)S(1)}, bf16[2,256,256]{2,1,0:T(8,128)(2,1)S(1)}, u32[]{:S(2)}, u32[]{:S(2)}) collective-permute-start(bf16[2,256,256]{2,1,0:T(8,128)(2,1)S(1)} %bitcast.26), channel_id=1, source_target_pairs={{0,8},{4,12},{8,0},{12,4},{1,9},{5,13},{9,1},{13,5},{2,10},{6,14},... | collective-permute-start | bytes 786440 | tf_op jit(solution)/shard_map/ppermute | solution.py:172
  6.1 1.6 %collective-permute-start.4 = (bf16[2,256,256]{2,1,0:T(8,128)(2,1)S(1)}, bf16[2,256,256]{2,1,0:T(8,128)(2,1)S(1)}, u32[]{:S(2)}, u32[]{:S(2)}) collective-permute-start(bf16[2,256,256]{2,1,0:T(8,128)(2,1)S(1)} %bitcast.27), channel_id=1, source_target_pairs={{0,4},{4,0},{8,12},{12,8},{1,5},{5,1},{9,13},{13,9},{2,6},{6,2},{1... | collective-permute-start | bytes 786440 | tf_op jit(solution)/shard_map/ppermute | solution.py:172
  7.7 11.0 %collective-permute-done.2.refs_3_ = bf16[2,256,256]{2,1,0:T(8,128)(2,1)S(1)} collective-permute-done((bf16[2,256,256]{2,1,0:T(8,128)(2,1)S(1)}, bf16[2,256,256]{2,1,0:T(8,128)(2,1)S(1)}, u32[]{:S(2)}, u32[]{:S(2)}) %collective-permute-start.2) | collective-permute-done | bytes 262176 | tf_op jit(solution)/shard_map/ppermute | solution.py:172
  18.8 0.7 %collective-permute-start.6 = (bf16[2,256,256]{2,1,0:T(8,128)(2,1)S(1)}, bf16[2,256,256]{2,1,0:T(8,128)(2,1)S(1)}, u32[]{:S(2)}, u32[]{:S(2)}) collective-permute-start(bf16[2,256,256]{2,1,0:T(8,128)(2,1)S(1)} %collective-permute-done.2.refs_3_), channel_id=1, source_target_pairs={{0,4},{4,0},{8,12},{12,8},{1,5},{5,1},{9,13},{13,9},{2,6},{6,2},{1... | collective-permute-start | bytes 786440 | tf_op jit(solution)/shard_map/ppermute | solution.py:172
  19.4 0.0 collective-permute-start
  19.4 1.4 %collective-permute-done = bf16[16,8,4,4]{0,3,2,1:T(4,128)(2,1)S(1)} collective-permute-done((bf16[16,8,4,4]{0,3,2,1:T(4,128)(2,1)}, bf16[16,8,4,4]{0,3,2,1:T(4,128)(2,1)S(1)}, u32[]{:S(2)}, u32[]{:S(2)}) %collective-permute-start) | collective-permute-done | bytes 4128 | tf_op jit(solution)/shard_map/ppermute | solution.py:193
  20.8 0.8 %maximum_bitcast_fusion = bf16[16,4,4,16]{0,1,2,3:T(4,128)(2,1)S(1)} fusion(bf16[16,8,4,4]{0,3,2,1:T(4,128)(2,1)S(1)} %collective-permute-done, bf16[16,8,4,4]{0,3,2,1:T(4,128)(2,1)} %param.9), kind=kLoop, calls=%fused_computation.2 | loop fusion | flops 4096 | bytes 16384 | tf_op jit(solution)/shard_map/transpose | solution.py:195
  21.6 0.1 copy.8
  21.8 0.2 collective-permute-start.3
  22.0 0.0 collective-permute-done.4.refs_3_
  22.0 0.3 collective-permute-start.5
  22.4 4.4 %collective-permute-done.6.refs_4_ = bf16[2,256,256]{2,1,0:T(8,128)(2,1)S(1)} collective-permute-done((bf16[2,256,256]{2,1,0:T(8,128)(2,1)S(1)}, bf16[2,256,256]{2,1,0:T(8,128)(2,1)S(1)}, u32[]{:S(2)}, u32[]{:S(2)}) %collective-permute-start.6) | collective-permute-done | bytes 262176 | tf_op jit(solution)/shard_map/ppermute | solution.py:172
  26.8 0.0 collective-permute-done.1.other_ref
  26.8 1.2 %copy-done.1 = bf16[8,256,256]{2,1,0:T(8,128)(2,1)S(1)} copy-done((bf16[8,256,256]{2,1,0:T(8,128)(2,1)S(1)}, bf16[8,256,256]{2,1,0:T(8,128)(2,1)}, u32[]{:S(2)}) %copy-start.1) | copy-done | bytes 1048600
  28.0 8.8 %mix_right.1 = bf16[64,16,16,512]{3,2,1,0:T(8,128)(2,1)S(1)} custom-call(bf16[256,16]{1,0:T(8,128)(2,1)S(1)} %bitcast.31, bf16[8,256,256]{2,1,0:T(8,128)(2,1)S(1)} %copy-done.1, bf16[8,256,256]{2,1,0:T(8,128)(2,1)} %collective-permute-done.1.other_ref), custom_call_target="tpu_custom_call" | custom-call | flops 4294967296 | bytes 16777216 | tf_op jit(solution)/shard_map/mix_right/pallas_call | solution.py:64
  36.8 4.0 %apply_block.4.refs_0_ = f32[256,512]{1,0:T(8,128)S(1)} custom-call(s32[16]{0:T(128)S(1)} %copy-done.2, s32[4]{0:T(128)S(1)} %copy-done.3, bf16[16,256,256]{2,1,0:T(8,128)(2,1)S(1)} %bitcast.22, bf16[16,1024,512]{2,1,0:T(8,128)(2,1)S(1)} %bitcast.18, bf16[2,256,256]{2,1,0:T(8,128)(2,1)S(1)} %bitcast.28, bf16[2,256,256]{2,1,0:T(8,128)(2,1)S(1)} %bitcast.29), custom_call_target="tpu_custom_call" | custom-call | flops 2013265920 | bytes 1048576 | tf_op jit(solution)/shard_map/apply_block/pallas_call | solution.py:143
  40.8 0.0 copy-start.4
  40.8 0.0 collective-permute-done.3.refs_4_
  40.8 5.3 %apply_block.5.refs_0_ = f32[256,512]{1,0:T(8,128)S(1)} custom-call(s32[16]{0:T(128)S(1)} %copy-done.2, s32[4]{0:T(128)S(1)} %copy-done.3, f32[256,512]{1,0:T(8,128)S(1)} %apply_block.4.refs_0_, bf16[16,256,256]{2,1,0:T(8,128)(2,1)S(1)} %bitcast.23, bf16[16,1024,512]{2,1,0:T(8,128)(2,1)S(1)} %bitcast.19, ...), custom_call_target="tpu_custom_call" | custom-call | flops 2013265920 | bytes 1048576 | tf_op jit(solution)/shard_map/apply_block/pallas_call | solution.py:143
  46.2 3.4 %apply_block.6.refs_1_ = f32[256,512]{1,0:T(8,128)S(1)} custom-call(s32[16]{0:T(128)S(1)} %copy-done.2, s32[4]{0:T(128)S(1)} %copy-done.3, f32[256,512]{1,0:T(8,128)S(1)} %apply_block.5.refs_0_, bf16[16,256,256]{2,1,0:T(8,128)(2,1)S(1)} %bitcast.24, bf16[16,1024,512]{2,1,0:T(8,128)(2,1)S(1)} %bitcast.20, ...), custom_call_target="tpu_custom_call" | custom-call | flops 2013265920 | bytes 1048576 | tf_op jit(solution)/shard_map/apply_block/pallas_call | solution.py:143
  49.6 0.8 %apply_block.7 = bf16[2,256,256]{2,1,0:T(8,128)(2,1)S(1)} custom-call(s32[16]{0:T(128)S(1)} %copy-done.2, s32[4]{0:T(128)S(1)} %copy-done.3, s32[4]{0:T(128)S(1)} %copy-done.4, f32[256,512]{1,0:T(8,128)S(1)} %apply_block.6.refs_1_, bf16[16,256,256]{2,1,0:T(8,128)(2,1)S(1)} %bitcast.25, bf16[16,1024,512]{2,1,0:T(8,128)(2,1)S(1)} %bitcast.21, ...), custom_call_target="tpu_custom_call" | custom-call | flops 2013265920 | bytes 1048576 | tf_op jit(solution)/shard_map/apply_block/pallas_call | solution.py:143
  50.5 1.0 %copy.11 = bf16[1,256,2,256]{3,2,1,0:T(2,128)(2,1)} copy(bf16[1,256,2,256]{3,1,2,0:T(8,128)(2,1)S(1)} %bitcast.30) | data formatting | bytes 524288 | tf_op jit(solution)/shard_map/broadcast_in_dim | solution.py:212
  (13 shorter events, 0.1 us)
Async XLA Ops:
  0.0 36.7 %copy-start = (bf16[16,1,256,256]{3,2,1,0:T(8,128)(2,1)S(1)}, bf16[16,1,256,256]{3,2,1,0:T(8,128)(2,1)}, u32[]{:S(2)}) copy-start(bf16[16,1,256,256]{3,2,1,0:T(8,128)(2,1)} %param.8) | copy-start | bytes 6291460
  0.0 36.8 %copy-start.2 = (s32[16]{0:T(128)S(1)}, s32[16]{0:T(128)}, u32[]{:S(2)}) copy-start(s32[16]{0:T(128)} %charges_ref.7) | copy-start | bytes 196
  0.0 36.8 %copy-start.3 = (s32[4]{0:T(128)S(1)}, s32[4]{0:T(128)}, u32[]{:S(2)}) copy-start(s32[4]{0:T(128)} %order_ref.7) | copy-start | bytes 52
  0.0 26.7 %collective-permute-start.1 = (bf16[8,256,256]{2,1,0:T(8,128)(2,1)}, bf16[8,256,256]{2,1,0:T(8,128)(2,1)}, u32[]{:S(2)}, u32[]{:S(2)}) collective-permute-start(bf16[8,256,256]{2,1,0:T(8,128)(2,1)} %own_ref.1), channel_id=1, source_target_pairs={{0,1},{1,0},{2,3},{3,2},{4,5},{5,4},{6,7},{7,6},{8,9},{9,8},{10,11... | collective-permute-start | bytes 3145736 | tf_op jit(solution)/shard_map/ppermute | solution.py:192
  2.4 16.3 %collective-permute-start.2 = (bf16[2,256,256]{2,1,0:T(8,128)(2,1)S(1)}, bf16[2,256,256]{2,1,0:T(8,128)(2,1)S(1)}, u32[]{:S(2)}, u32[]{:S(2)}) collective-permute-start(bf16[2,256,256]{2,1,0:T(8,128)(2,1)S(1)} %bitcast.26), channel_id=1, source_target_pairs={{0,8},{4,12},{8,0},{12,4},{1,9},{5,13},{9,1},{13,5},{2,10},{6,14},... | collective-permute-start | bytes 786440 | tf_op jit(solution)/shard_map/ppermute | solution.py:172
  6.1 15.9 %collective-permute-start.4 = (bf16[2,256,256]{2,1,0:T(8,128)(2,1)S(1)}, bf16[2,256,256]{2,1,0:T(8,128)(2,1)S(1)}, u32[]{:S(2)}, u32[]{:S(2)}) collective-permute-start(bf16[2,256,256]{2,1,0:T(8,128)(2,1)S(1)} %bitcast.27), channel_id=1, source_target_pairs={{0,4},{4,0},{8,12},{12,8},{1,5},{5,1},{9,13},{13,9},{2,6},{6,2},{1... | collective-permute-start | bytes 786440 | tf_op jit(solution)/shard_map/ppermute | solution.py:172
  18.8 8.0 %collective-permute-start.6 = (bf16[2,256,256]{2,1,0:T(8,128)(2,1)S(1)}, bf16[2,256,256]{2,1,0:T(8,128)(2,1)S(1)}, u32[]{:S(2)}, u32[]{:S(2)}) collective-permute-start(bf16[2,256,256]{2,1,0:T(8,128)(2,1)S(1)} %collective-permute-done.2.refs_3_), channel_id=1, source_target_pairs={{0,4},{4,0},{8,12},{12,8},{1,5},{5,1},{9,13},{13,9},{2,6},{6,2},{1... | collective-permute-start | bytes 786440 | tf_op jit(solution)/shard_map/ppermute | solution.py:172
  19.4 1.4 %collective-permute-start = (bf16[16,8,4,4]{0,3,2,1:T(4,128)(2,1)}, bf16[16,8,4,4]{0,3,2,1:T(4,128)(2,1)S(1)}, u32[]{:S(2)}, u32[]{:S(2)}) collective-permute-start(bf16[16,8,4,4]{0,3,2,1:T(4,128)(2,1)} %param.9), channel_id=1, source_target_pairs={{0,1},{1,0},{2,3},{3,2},{4,5},{5,4},{6,7},{7,6},{8,9},{9,8},{10,11... | collective-permute-start | bytes 12296 | tf_op jit(solution)/shard_map/ppermute | solution.py:193
  21.8 19.0 %collective-permute-start.3 = (bf16[2,256,256]{2,1,0:T(8,128)(2,1)S(1)}, bf16[2,256,256]{2,1,0:T(8,128)(2,1)S(1)}, u32[]{:S(2)}, u32[]{:S(2)}) collective-permute-start(bf16[2,256,256]{2,1,0:T(8,128)(2,1)S(1)} %collective-permute-done.2.refs_3_), channel_id=1, source_target_pairs={{0,1},{1,0},{2,3},{3,2},{4,5},{5,4},{6,7},{7,6},{8,9},{9,8},{10,11... | collective-permute-start | bytes 786440 | tf_op jit(solution)/shard_map/ppermute | solution.py:206
  22.0 24.2 %collective-permute-start.5 = (bf16[2,256,256]{2,1,0:T(8,128)(2,1)S(1)}, bf16[2,256,256]{2,1,0:T(8,128)(2,1)S(1)}, u32[]{:S(2)}, u32[]{:S(2)}) collective-permute-start(bf16[2,256,256]{2,1,0:T(8,128)(2,1)S(1)} %collective-permute-done.4.refs_3_), channel_id=1, source_target_pairs={{0,1},{1,0},{2,3},{3,2},{4,5},{5,4},{6,7},{7,6},{8,9},{9,8},{10,11... | collective-permute-start | bytes 786440 | tf_op jit(solution)/shard_map/ppermute | solution.py:206
  26.7 22.8 %collective-permute-start.7 = (bf16[2,256,256]{2,1,0:T(8,128)(2,1)S(1)}, bf16[2,256,256]{2,1,0:T(8,128)(2,1)S(1)}, u32[]{:S(2)}, u32[]{:S(2)}) collective-permute-start(bf16[2,256,256]{2,1,0:T(8,128)(2,1)S(1)} %collective-permute-done.6.refs_4_), channel_id=1, source_target_pairs={{0,1},{1,0},{2,3},{3,2},{4,5},{5,4},{6,7},{7,6},{8,9},{9,8},{10,11... | collective-permute-start | bytes 786440 | tf_op jit(solution)/shard_map/ppermute | solution.py:206
  26.8 1.2 %copy-start.1 = (bf16[8,256,256]{2,1,0:T(8,128)(2,1)S(1)}, bf16[8,256,256]{2,1,0:T(8,128)(2,1)}, u32[]{:S(2)}) copy-start(bf16[8,256,256]{2,1,0:T(8,128)(2,1)} %own_ref.1) | copy-start | bytes 3145732
  40.8 8.8 %copy-start.4 = (s32[4]{0:T(128)S(1)}, s32[4]{0:T(128)}, u32[]{:S(2)}) copy-start(s32[4]{0:T(128)} %refs_0_.1) | copy-start | bytes 52
where the time goes:
time: 51.8 us; the launch traced here: 51.4 us
  Pallas kernels  22.3 us (43%)
  waiting for transfers between devices  16.8 us (32%)
  starting transfers between devices  7.07 us (14%)
  local copies, waits for them, and re-layouts  4.25 us (8%)
  other arithmetic  0.81 us (2%)
    ppermute x3, waiting for transfers between devices, gather_blocks(): blocks[hop | bit] = lax.ppermute(blocks[hop], axis, pairs)  15.4 us
    pallas_call x4, Pallas kernels, apply_block(): pl.pallas_call(kernel, out_shape=out_shape, in_specs=[SMEM_SPEC] * len(sc...  13.6 us
    pallas_call x1, Pallas kernels, mix_right(): pl.pallas_call(kernel, out_shape=jax.ShapeDtypeStruct((groups, row_tiles,...  8.75 us
    ppermute x3, starting transfers between devices, gather_blocks(): blocks[hop | bit] = lax.ppermute(blocks[hop], axis, pairs)  5.93 us
    another operation x3, local copies, waits for them, and re-layouts  1.89 us
    ppermute x1, waiting for transfers between devices, step(): mpo_other = lax.ppermute(mpo_terms, 'gz', swap)  1.38 us
    unnamed x10, local copies, waits for them, and re-layouts  1.24 us
  transfers between devices with their start and end apart: 8, of which 3 were waited for; matrix products, arithmetic and copies ran while one was open for 6% of the time, Pallas kernels for 42%

commit v1 on v0

v1 whole, which is shorter than its diff:
```python
import jax
import jax.numpy as jnp
from jax import lax
from jax.experimental import pallas as pl
from jax.experimental.pallas import tpu as pltpu
from jax.sharding import PartitionSpec as P


LANE_ROWS = 16
MIX_ROWS = 512
MIX_TILES = 8
BF16 = jnp.bfloat16
F32 = jnp.float32
VMEM_SPEC = pl.BlockSpec(memory_space=pltpu.VMEM)
SMEM_SPEC = pl.BlockSpec(memory_space=pltpu.SMEM)


def dot(a, b):
    return jnp.dot(a, b, preferred_element_type=F32)


def iota(shape, axis):
    return lax.broadcasted_iota(jnp.int32, shape, axis)


def mix_right(mpo_rows, right_own, right_other, terms, phys, phys_own):
    share, rows, cols = right_own.shape
    right_count = 2 * share
    depth = right_count * LANE_ROWS
    groups = terms * phys
    lhs_rows = groups * phys_own * LANE_ROWS
    width = MIX_TILES * LANE_ROWS
    steps = rows // width
    chunk = min(lhs_rows, MIX_ROWS)

    def kernel(mpo_ref, own_hbm, other_hbm, out_ref, lhs, own_ref, other_ref, sems):
        core = lax.axis_index("gz")
        copies = [
            pltpu.make_async_copy(source, target, sems.at[i])
            for i, (source, target) in enumerate([(own_hbm, own_ref), (other_hbm, other_ref)])
        ]
        for copy in copies:
            copy.start()
        shape = (groups * phys_own, groups * phys)
        row = iota(shape, 0)
        wanted = (row // phys_own) * phys + core * phys_own + row % phys_own
        pick = (iota(shape, 1) == wanted).astype(F32).astype(BF16)
        picked = dot(pick, mpo_ref[...]).astype(BF16)
        widen = iota((right_count, depth), 1) // LANE_ROWS == iota((right_count, depth), 0)
        wide = dot(picked, widen.astype(F32).astype(BF16))
        shape = (LANE_ROWS, depth)
        same = (iota(shape, 0) == iota(shape, 1) % LANE_ROWS).astype(F32)
        tall = wide[:, None, :] * same[None, :, :]
        lhs[...] = tall.reshape(lhs_rows, depth).astype(BF16)
        for copy in copies:
            copy.wait()

        def tile(step, carry):
            parts = []
            for t in range(MIX_TILES):
                begin = pl.multiple_of(step * width + t * LANE_ROWS, LANE_ROWS)
                here = pl.ds(begin, LANE_ROWS)
                sides = [ref[:, here, :].reshape(-1, cols) for ref in (own_ref, other_ref)]
                parts.append(jnp.concatenate(sides, 0))
            rhs = jnp.concatenate(parts, 1)
            for start in range(0, lhs_rows, chunk):
                part = dot(lhs[start : start + chunk, :], rhs).astype(BF16)
                part = part.reshape(chunk // LANE_ROWS, LANE_ROWS, MIX_TILES * cols)
                for i in range(chunk // LANE_ROWS):
                    group, p = divmod(start // LANE_ROWS + i, phys_own)
                    for t in range(MIX_TILES):
                        out_ref[group, step * MIX_TILES + t, :, p * cols : (p + 1) * cols] = part[
                            i, :, t * cols : (t + 1) * cols
                        ]
            return carry

        lax.fori_loop(0, steps, tile, 0)

    row_tiles = rows // LANE_ROWS
    out = pl.pallas_call(
        kernel,
        out_shape=jax.ShapeDtypeStruct((groups, row_tiles, LANE_ROWS, phys_own * cols), BF16),
        in_specs=[VMEM_SPEC, pl.BlockSpec(memory_space=pl.ANY), pl.BlockSpec(memory_space=pl.ANY)],
        out_specs=VMEM_SPEC,
        scratch_shapes=[
            pltpu.VMEM((lhs_rows, depth), BF16),
            pltpu.VMEM(right_own.shape, BF16),
            pltpu.VMEM(right_own.shape, BF16),
            pltpu.SemaphoreType.DMA((2,)),
        ],
        compiler_params=pltpu.CompilerParams(vmem_limit_bytes=20 << 20),
        cost_estimate=pl.CostEstimate(
            flops=2 * lhs_rows * depth * cols * row_tiles,
            bytes_accessed=2 * groups * rows * phys_own * cols,
            transcendentals=0,
        ),
        name="mix_right",
    )(mpo_rows, right_own, right_other)
    return out.reshape(terms, phys * rows, phys_own * cols)


def apply_blocks(hops, partner, blocks, total, left, mixed, charges, order, dims=None):
    terms, rows, depth = left.shape
    out_cols = mixed.shape[2]
    half, _, cols = blocks[0].shape
    first, last = total is None, dims is not None

    def kernel(charges_ref, order_ref, *refs):
        refs = list(refs)
        dims_ref = refs.pop(0) if last else None
        total_ref = None if first else refs.pop(0)
        left_ref, mixed_ref = refs[:2]
        block_refs = refs[2 : 2 + len(blocks)]
        out_ref, term_list, block_list, sources = refs[2 + len(blocks) :][:4]
        acc = refs[-1] if last else out_ref
        me, core = lax.axis_index("gx"), lax.axis_index("gz")
        count = jnp.int32(0)
        for i, hop in enumerate(hops):
            shift = order_ref[partner(me, hop)] - order_ref[me] + 1
            for u in range(terms):
                term_list[count] = u
                block_list[count] = i
                count += (charges_ref[u] == shift).astype(jnp.int32)
            for q in range(half):
                sources[i, core * half + q] = block_refs[2 * i][q]
                sources[i, (1 - core) * half + q] = block_refs[2 * i + 1][q]
        acc[...] = jnp.zeros_like(acc) if first else total_ref[...]

        def add(start, many):
            sums = None
            for k in range(many):
                u, i = term_list[start + k], block_list[start + k]
                env = left_ref[u]
                applied = [dot(env, sources[i, q]).astype(BF16) for q in range(2 * half)]
                piece = dot(jnp.concatenate(applied, 1), mixed_ref[u])
                sums = piece if sums is None else sums + piece
            acc[...] += sums

        def four(i, carry):
            add(4 * i, 4)
            return carry

        lax.fori_loop(0, count // 4, four, 0)
        rest = count % 4

        @pl.when(rest >= 2)
        def _():
            add(count - rest, 2)

        @pl.when(rest % 2 == 1)
        def _():
            add(count - 1, 1)

        if last:
            keep = iota((rows, out_cols), 0) < dims_ref[me]
            masked = jnp.where(keep, acc[...], 0.0)
            out_ref[...] = masked.reshape(rows, out_cols // cols, cols).astype(BF16)

    slots = terms * len(hops) + 1
    scratch = [
        pltpu.SMEM((slots,), jnp.int32),
        pltpu.SMEM((slots,), jnp.int32),
        pltpu.VMEM((len(hops), 2 * half, depth, cols), BF16),
    ]
    if last:
        scratch.append(pltpu.VMEM((rows, out_cols), F32))
        out_shape = jax.ShapeDtypeStruct((rows, out_cols // cols, cols), BF16)
    else:
        out_shape = jax.ShapeDtypeStruct((rows, out_cols), F32)
    scalars = [charges, order] + ([dims] if last else [])
    arrays = ([] if first else [total]) + [left, mixed] + list(blocks)
    block_bytes = 2 * depth * half * 2 * cols
    return pl.pallas_call(
        kernel,
        out_shape=out_shape,
        in_specs=[SMEM_SPEC] * len(scalars) + [VMEM_SPEC] * len(arrays),
        out_specs=VMEM_SPEC,
        scratch_shapes=scratch,
        compiler_params=pltpu.CompilerParams(
            vmem_limit_bytes=(8 << 20) + 2 * len(hops) * block_bytes
        ),
        cost_estimate=pl.CostEstimate(
            flops=2 * (terms // 3) * rows * 2 * half * cols * len(hops) * (depth + out_cols),
            bytes_accessed=2 * rows * out_cols * 4,
            transcendentals=0,
        ),
        name="apply_blocks",
    )(*scalars, *arrays)


def gather_blocks(own, axis):
    count = lax.axis_size(axis)
    if count & (count - 1):
        blocks = {}
        for hop in range(1, count):
            pairs = [(i, (i + hop) % count) for i in range(count)]
            blocks[hop] = lax.ppermute(own, axis, pairs)
        return blocks, lambda me, hop: lax.rem(me - hop + count, count)
    blocks = {0: own}
    bit = count // 2
    while bit:
        pairs = [(i, i ^ bit) for i in range(count)]
        for hop in list(blocks):
            blocks[hop | bit] = lax.ppermute(blocks[hop], axis, pairs)
        bit //= 2
    del blocks[0]
    return blocks, lambda me, hop: lax.bitwise_xor(me, hop)


def use_stages(count):
    order = sorted(range(1, count), key=lambda hop: (bin(hop).count("1"), -hop))
    return [hops for hops in ([0] + order[:-1], order[-1:]) if hops]


def step(state, left_env, mpo_terms, right_env, term_charge, charge_order, sector_dims):
    terms, share, phys, _ = mpo_terms.shape
    cores = lax.axis_size("gz")
    assert state.shape[0] == 1 and cores == 2
    half = phys // cores
    core = lax.axis_index("gz")
    swap = [(0, 1), (1, 0)]
    planes = state[0].transpose(1, 0, 2)
    own = lax.dynamic_slice_in_dim(planes, core * half, half, 0)
    blocks, partner = gather_blocks(own, "gx")
    right_other = lax.ppermute(right_env, "gz", swap)
    mpo_other = lax.ppermute(mpo_terms, "gz", swap)
    mpo_all = jnp.concatenate([mpo_terms, mpo_other], 1)
    mpo_rows = mpo_all.transpose(0, 3, 2, 1).reshape(terms * phys * phys, cores * share)
    mixed = mix_right(mpo_rows, right_env, right_other, terms, phys, half)
    left = left_env[:, 0]

    own_other = lax.dynamic_slice_in_dim(planes, (1 - core) * half, half, 0)
    pairs = {0: (own, own_other)}
    for hop, block in blocks.items():
        pairs[hop] = (block, lax.ppermute(block, "gz", swap))
    total = None
    stages = use_stages(lax.axis_size("gx"))
    for number, hops in enumerate(stages):
        dims = sector_dims if number == len(stages) - 1 else None
        parts = [part for hop in hops for part in pairs[hop]]
        total = apply_blocks(
            hops, partner, parts, total, left, mixed, term_charge, charge_order, dims
        )
    return total[None]


def solution(mesh):
    return jax.shard_map(
        step,
        mesh=mesh,
        in_specs=(
            P(("ga", "gx"), None, None, "gy"),
            P(None, ("ga", "gx"), None, None),
            P(None, "gz", None, None),
            P("gz", ("ga", "gy"), None),
            P(),
            P("ga"),
            P("ga"),
        ),
        out_specs=P(("ga", "gx"), None, "gz", "gy"),
        check_vma=False,
    )
```

time: 51.8 us -> 44.9 us (0.87)
  Pallas kernels: 22.3 us -> 15.6 us
    pallas_call x1, Pallas kernels: 8.75 us -> 5.29 us  [mix_right(): pl.pallas_call(kernel, out_shape=jax.ShapeDtypeStruct((groups, row_tiles,...]
    pallas_call x4 -> x2, Pallas kernels: 13.6 us -> 10.3 us  [apply_blocks(): pl.pallas_call(kernel, out_shape=out_shape, in_specs=[SMEM_SPEC] * len(sc...]
    another operation x3, local copies, waits for them, and re-layouts: 1.89 us -> 3.31 us
    broadcast_in_dim x1 -> x0, local copies, waits for them, and re-layouts: 0.97 us -> none  [step(): return total.transpose(1, 0, 2)[None]]
    ppermute x1, waiting for transfers between devices: 1.38 us -> 0.67 us  [step(): mpo_other = lax.ppermute(mpo_terms, 'gz', swap)]
    unnamed x10 -> x12, local copies, waits for them, and re-layouts: 1.24 us -> 1.24 us
  transfers between devices with their start and end apart: 8 -> 8, of which waited for: 3 -> 3; matrix products, arithmetic and copies ran while one was open for 6% -> 10% of each run, Pallas kernels for 42% -> 31%
where the time goes in v1:
time: 44.9 us; the launch traced here: 44.7 us
  waiting for transfers between devices  16.5 us (37%)
  Pallas kernels  15.6 us (35%)
  starting transfers between devices  6.98 us (16%)
  local copies, waits for them, and re-layouts  4.7 us (10%)
  other arithmetic  0.81 us (2%)
    ppermute x3, waiting for transfers between devices, gather_blocks(): blocks[hop | bit] = lax.ppermute(blocks[hop], axis, pairs)  15.8 us
    pallas_call x2, Pallas kernels, apply_blocks(): pl.pallas_call(kernel, out_shape=out_shape, in_specs=[SMEM_SPEC] * len(sc...  10.3 us
    ppermute x3, starting transfers between devices, gather_blocks(): blocks[hop | bit] = lax.ppermute(blocks[hop], axis, pairs)  5.84 us
    pallas_call x1, Pallas kernels, mix_right(): pl.pallas_call(kernel, out_shape=jax.ShapeDtypeStruct((groups, row_tiles,...  5.29 us
    another operation x3, local copies, waits for them, and re-layouts  3.31 us
    unnamed x12, local copies, waits for them, and re-layouts  1.24 us
  transfers between devices with their start and end apart: 8, of which 3 were waited for; matrix products, arithmetic and copies ran while one was open for 10% of the time, Pallas kernels for 31%

profile of v1, /device:TPU:0, one launch (start us, length us, event | category | flops | bytes accessed | tf_op | source)
XLA Modules:
  0.0 44.7 jit_solution(2505593351376287211)
XLA Ops:
  0.0 0.6 %collective-permute-start.1 = (bf16[8,256,256]{2,1,0:T(8,128)(2,1)}, bf16[8,256,256]{2,1,0:T(8,128)(2,1)S(1)}, u32[]{:S(2)}, u32[]{:S(2)}) collective-permute-start(bf16[8,256,256]{2,1,0:T(8,128)(2,1)} %own_hbm.1), channel_id=1, source_target_pairs={{0,1},{1,0},{2,3},{3,2},{4,5},{5,4},{6,7},{7,6},{8,9},{9,8},{10,11... | collective-permute-start | bytes 3145736 | tf_op jit(solution)/shard_map/ppermute | solution.py:225
  0.6 1.8 %constant_dynamic-slice_fusion = (bf16[1,256,2,256]{3,2,1,0:T(2,128)(2,1)S(1)}, bf16[1,256,2,256]{3,2,1,0:T(2,128)(2,1)S(1)}) fusion(bf16[1,256,4,256]{3,2,1,0:T(4,128)(2,1)} %param.7, s32[]{:T(128)S(6)} %select_n.7, s32[]{:T(128)S(6)} %select_n.6), kind=kLoop, calls=%fused_computation.3 | loop fusion | bytes 1048584 | tf_op jit(solution)/shard_map/dynamic-slice.3
  2.4 0.7 %copy.14 = bf16[1,256,2,256]{3,1,2,0:T(8,128)(2,1)} copy(bf16[1,256,2,256]{3,2,1,0:T(2,128)(2,1)S(1)} %get-tuple-element.6) | data formatting | bytes 524288 | tf_op jit(solution)/shard_map/dynamic-slice.2
  3.1 3.6 %collective-permute-start.2 = (bf16[2,256,256]{2,1,0:T(8,128)(2,1)}, bf16[2,256,256]{2,1,0:T(8,128)(2,1)}, u32[]{:S(2)}, u32[]{:S(2)}) collective-permute-start(bf16[2,256,256]{2,1,0:T(8,128)(2,1)} %bitcast.15.refs_2_), channel_id=1, source_target_pairs={{0,8},{4,12},{8,0},{12,4},{1,9},{5,13},{9,1},{13,5},{2,10},{6,14},... | collective-permute-start | bytes 786440 | tf_op jit(solution)/shard_map/ppermute | solution.py:204
  6.8 1.6 %collective-permute-start.4 = (bf16[2,256,256]{2,1,0:T(8,128)(2,1)}, bf16[2,256,256]{2,1,0:T(8,128)(2,1)}, u32[]{:S(2)}, u32[]{:S(2)}) collective-permute-start(bf16[2,256,256]{2,1,0:T(8,128)(2,1)} %bitcast.15.refs_2_), channel_id=1, source_target_pairs={{0,4},{4,0},{8,12},{12,8},{1,5},{5,1},{9,13},{13,9},{2,6},{6,2},{1... | collective-permute-start | bytes 786440 | tf_op jit(solution)/shard_map/ppermute | solution.py:204
  8.4 11.3 %collective-permute-done.2.refs_4_ = bf16[2,256,256]{2,1,0:T(8,128)(2,1)} collective-permute-done((bf16[2,256,256]{2,1,0:T(8,128)(2,1)}, bf16[2,256,256]{2,1,0:T(8,128)(2,1)}, u32[]{:S(2)}, u32[]{:S(2)}) %collective-permute-start.2) | collective-permute-done | bytes 262176 | tf_op jit(solution)/shard_map/ppermute | solution.py:204
  19.6 0.6 %collective-permute-start.6 = (bf16[2,256,256]{2,1,0:T(8,128)(2,1)}, bf16[2,256,256]{2,1,0:T(8,128)(2,1)S(1)}, u32[]{:S(2)}, u32[]{:S(2)}) collective-permute-start(bf16[2,256,256]{2,1,0:T(8,128)(2,1)} %collective-permute-done.2.refs_4_), channel_id=1, source_target_pairs={{0,4},{4,0},{8,12},{12,8},{1,5},{5,1},{9,13},{13,9},{2,6},{6,2},{1... | collective-permute-start | bytes 786440 | tf_op jit(solution)/shard_map/ppermute | solution.py:204
  20.3 0.0 collective-permute-start
  20.3 0.7 %copy.13 = bf16[1,256,2,256]{3,1,2,0:T(8,128)(2,1)} copy(bf16[1,256,2,256]{3,2,1,0:T(2,128)(2,1)S(1)} %get-tuple-element.5) | data formatting | bytes 524288 | tf_op jit(solution)/shard_map/dynamic-slice.3
  21.0 0.7 %collective-permute-done = bf16[16,8,4,4]{0,3,2,1:T(4,128)(2,1)S(1)} collective-permute-done((bf16[16,8,4,4]{0,3,2,1:T(4,128)(2,1)}, bf16[16,8,4,4]{0,3,2,1:T(4,128)(2,1)S(1)}, u32[]{:S(2)}, u32[]{:S(2)}) %collective-permute-start) | collective-permute-done | bytes 4128 | tf_op jit(solution)/shard_map/ppermute | solution.py:226
  21.7 0.8 %maximum_bitcast_fusion = bf16[16,4,4,16]{0,1,2,3:T(4,128)(2,1)S(1)} fusion(bf16[16,8,4,4]{0,3,2,1:T(4,128)(2,1)S(1)} %collective-permute-done, bf16[16,8,4,4]{0,3,2,1:T(4,128)(2,1)} %param.9), kind=kLoop, calls=%fused_computation.2 | loop fusion | flops 4096 | bytes 16384 | tf_op jit(solution)/shard_map/transpose | solution.py:228
  22.5 0.1 copy.8
  22.6 0.2 collective-permute-start.3
  22.9 0.0 collective-permute-done.4.refs_6_
  22.9 0.3 collective-permute-start.5
  23.2 4.6 %collective-permute-done.6.refs_4_ = bf16[2,256,256]{2,1,0:T(8,128)(2,1)S(1)} collective-permute-done((bf16[2,256,256]{2,1,0:T(8,128)(2,1)}, bf16[2,256,256]{2,1,0:T(8,128)(2,1)S(1)}, u32[]{:S(2)}, u32[]{:S(2)}) %collective-permute-start.6) | collective-permute-done | bytes 262176 | tf_op jit(solution)/shard_map/ppermute | solution.py:204
  27.8 0.0 collective-permute-start.7
  27.8 0.0 collective-permute-done.1.other_hbm
  27.8 1.2 %copy-done.1 = bf16[8,256,256]{2,1,0:T(8,128)(2,1)S(1)} copy-done((bf16[8,256,256]{2,1,0:T(8,128)(2,1)S(1)}, bf16[8,256,256]{2,1,0:T(8,128)(2,1)}, u32[]{:S(2)}) %copy-start.1) | copy-done | bytes 1048600
  29.0 5.3 %mix_right.1 = bf16[64,16,16,512]{3,2,1,0:T(8,128)(2,1)S(1)} custom-call(bf16[256,16]{1,0:T(8,128)(2,1)S(1)} %bitcast.20, bf16[8,256,256]{2,1,0:T(8,128)(2,1)S(1)} %copy-done.1, bf16[8,256,256]{2,1,0:T(8,128)(2,1)S(1)} %collective-permute-done.1.other_hbm), custom_call_target="tpu_custom_call" | custom-call | flops 4294967296 | bytes 16777216 | tf_op jit(solution)/shard_map/mix_right/pallas_call | solution.py:80
  34.3 0.0 collective-permute-done.3.refs_5_
  34.4 8.6 %apply_blocks.2.refs_1_ = f32[256,512]{1,0:T(8,128)S(1)} custom-call(s32[16]{0:T(128)S(1)} %copy-done.3, s32[4]{0:T(128)S(1)} %copy-done.4, bf16[16,256,256]{2,1,0:T(8,128)(2,1)S(1)} %bitcast.18, bf16[16,1024,512]{2,1,0:T(8,128)(2,1)S(1)} %bitcast.16, bf16[2,256,256]{2,1,0:T(8,128)(2,1)} %bitcast.15.refs_2_, bf16[2,256,256]{2,1,0:T(8,128)(2,1)S(1)} %bitcast.21, ...), custom_call_target="tpu_custom_call" | custom-call | flops 6039797760 | bytes 1048576 | tf_op jit(solution)/shard_map/apply_blocks/pallas_call | solution.py:173
  43.0 0.0 collective-permute-done.7.refs_5_
  43.0 1.6 %apply_blocks.3 = bf16[256,2,256]{2,1,0:T(2,128)(2,1)} custom-call(s32[16]{0:T(128)S(1)} %copy-done.3, s32[4]{0:T(128)S(1)} %copy-done.4, s32[4]{0:T(128)S(1)} %copy-done.5, f32[256,512]{1,0:T(8,128)S(1)} %apply_blocks.2.refs_1_, bf16[16,256,256]{2,1,0:T(8,128)(2,1)S(1)} %bitcast.19, bf16[16,1024,512]{2,1,0:T(8,128)(2,1)S(1)} %bitcast.17, ...), custom_call_target="tpu_custom_call" | custom-call | flops 2013265920 | bytes 1048576 | tf_op jit(solution)/shard_map/apply_blocks/pallas_call | solution.py:173
  (12 shorter events, 0.0 us)
Async XLA Ops:
  0.0 34.3 %copy-start.3 = (s32[16]{0:T(128)S(1)}, s32[16]{0:T(128)}, u32[]{:S(2)}) copy-start(s32[16]{0:T(128)} %charges_ref.3) | copy-start | bytes 196
  0.0 34.3 %copy-start.4 = (s32[4]{0:T(128)S(1)}, s32[4]{0:T(128)}, u32[]{:S(2)}) copy-start(s32[4]{0:T(128)} %order_ref.3) | copy-start | bytes 52
  0.0 34.3 %copy-start = (bf16[16,1,256,256]{3,2,1,0:T(8,128)(2,1)S(1)}, bf16[16,1,256,256]{3,2,1,0:T(8,128)(2,1)}, u32[]{:S(2)}) copy-start(bf16[16,1,256,256]{3,2,1,0:T(8,128)(2,1)} %param.8) | copy-start | bytes 6291460
  0.0 27.8 %collective-permute-start.1 = (bf16[8,256,256]{2,1,0:T(8,128)(2,1)}, bf16[8,256,256]{2,1,0:T(8,128)(2,1)S(1)}, u32[]{:S(2)}, u32[]{:S(2)}) collective-permute-start(bf16[8,256,256]{2,1,0:T(8,128)(2,1)} %own_hbm.1), channel_id=1, source_target_pairs={{0,1},{1,0},{2,3},{3,2},{4,5},{5,4},{6,7},{7,6},{8,9},{9,8},{10,11... | collective-permute-start | bytes 3145736 | tf_op jit(solution)/shard_map/ppermute | solution.py:225
  3.1 16.5 %collective-permute-start.2 = (bf16[2,256,256]{2,1,0:T(8,128)(2,1)}, bf16[2,256,256]{2,1,0:T(8,128)(2,1)}, u32[]{:S(2)}, u32[]{:S(2)}) collective-permute-start(bf16[2,256,256]{2,1,0:T(8,128)(2,1)} %bitcast.15.refs_2_), channel_id=1, source_target_pairs={{0,8},{4,12},{8,0},{12,4},{1,9},{5,13},{9,1},{13,5},{2,10},{6,14},... | collective-permute-start | bytes 786440 | tf_op jit(solution)/shard_map/ppermute | solution.py:204
  6.8 16.1 %collective-permute-start.4 = (bf16[2,256,256]{2,1,0:T(8,128)(2,1)}, bf16[2,256,256]{2,1,0:T(8,128)(2,1)}, u32[]{:S(2)}, u32[]{:S(2)}) collective-permute-start(bf16[2,256,256]{2,1,0:T(8,128)(2,1)} %bitcast.15.refs_2_), channel_id=1, source_target_pairs={{0,4},{4,0},{8,12},{12,8},{1,5},{5,1},{9,13},{13,9},{2,6},{6,2},{1... | collective-permute-start | bytes 786440 | tf_op jit(solution)/shard_map/ppermute | solution.py:204
  19.6 8.1 %collective-permute-start.6 = (bf16[2,256,256]{2,1,0:T(8,128)(2,1)}, bf16[2,256,256]{2,1,0:T(8,128)(2,1)S(1)}, u32[]{:S(2)}, u32[]{:S(2)}) collective-permute-start(bf16[2,256,256]{2,1,0:T(8,128)(2,1)} %collective-permute-done.2.refs_4_), channel_id=1, source_target_pairs={{0,4},{4,0},{8,12},{12,8},{1,5},{5,1},{9,13},{13,9},{2,6},{6,2},{1... | collective-permute-start | bytes 786440 | tf_op jit(solution)/shard_map/ppermute | solution.py:204
  20.3 1.4 %collective-permute-start = (bf16[16,8,4,4]{0,3,2,1:T(4,128)(2,1)}, bf16[16,8,4,4]{0,3,2,1:T(4,128)(2,1)S(1)}, u32[]{:S(2)}, u32[]{:S(2)}) collective-permute-start(bf16[16,8,4,4]{0,3,2,1:T(4,128)(2,1)} %param.9), channel_id=1, source_target_pairs={{0,1},{1,0},{2,3},{3,2},{4,5},{5,4},{6,7},{7,6},{8,9},{9,8},{10,11... | collective-permute-start | bytes 12296 | tf_op jit(solution)/shard_map/ppermute | solution.py:226
  22.6 11.7 %collective-permute-start.3 = (bf16[2,256,256]{2,1,0:T(8,128)(2,1)}, bf16[2,256,256]{2,1,0:T(8,128)(2,1)S(1)}, u32[]{:S(2)}, u32[]{:S(2)}) collective-permute-start(bf16[2,256,256]{2,1,0:T(8,128)(2,1)} %collective-permute-done.2.refs_4_), channel_id=1, source_target_pairs={{0,1},{1,0},{2,3},{3,2},{4,5},{5,4},{6,7},{7,6},{8,9},{9,8},{10,11... | collective-permute-start | bytes 786440 | tf_op jit(solution)/shard_map/ppermute | solution.py:235
  22.9 11.5 %collective-permute-start.5 = (bf16[2,256,256]{2,1,0:T(8,128)(2,1)}, bf16[2,256,256]{2,1,0:T(8,128)(2,1)S(1)}, u32[]{:S(2)}, u32[]{:S(2)}) collective-permute-start(bf16[2,256,256]{2,1,0:T(8,128)(2,1)} %collective-permute-done.4.refs_6_), channel_id=1, source_target_pairs={{0,1},{1,0},{2,3},{3,2},{4,5},{5,4},{6,7},{7,6},{8,9},{9,8},{10,11... | collective-permute-start | bytes 786440 | tf_op jit(solution)/shard_map/ppermute | solution.py:235
  27.8 15.2 %collective-permute-start.7 = (bf16[2,256,256]{2,1,0:T(8,128)(2,1)S(1)}, bf16[2,256,256]{2,1,0:T(8,128)(2,1)S(1)}, u32[]{:S(2)}, u32[]{:S(2)}) collective-permute-start(bf16[2,256,256]{2,1,0:T(8,128)(2,1)S(1)} %collective-permute-done.6.refs_4_), channel_id=1, source_target_pairs={{0,1},{1,0},{2,3},{3,2},{4,5},{5,4},{6,7},{7,6},{8,9},{9,8},{10,11... | collective-permute-start | bytes 786440 | tf_op jit(solution)/shard_map/ppermute | solution.py:235
  27.8 1.2 %copy-start.1 = (bf16[8,256,256]{2,1,0:T(8,128)(2,1)S(1)}, bf16[8,256,256]{2,1,0:T(8,128)(2,1)}, u32[]{:S(2)}) copy-start(bf16[8,256,256]{2,1,0:T(8,128)(2,1)} %own_hbm.1) | copy-start | bytes 3145732
  29.0 5.4 %copy-start.2 = (bf16[1,256,2,256]{3,1,2,0:T(8,128)(2,1)S(1)}, bf16[1,256,2,256]{3,1,2,0:T(8,128)(2,1)}, u32[]{:S(2)}) copy-start(bf16[1,256,2,256]{3,1,2,0:T(8,128)(2,1)} %copy.13) | copy-start | bytes 786436
  29.0 14.0 %copy-start.5 = (s32[4]{0:T(128)S(1)}, s32[4]{0:T(128)}, u32[]{:S(2)}) copy-start(s32[4]{0:T(128)} %refs_0_.1) | copy-start | bytes 52

commit v2 on v1

v2 whole, which is shorter than its diff:
```python
import jax
import jax.numpy as jnp
from jax import lax
from jax.experimental import pallas as pl
from jax.experimental.pallas import tpu as pltpu
from jax.sharding import PartitionSpec as P


LANE_ROWS = 16
MIX_ROWS = 512
MIX_TILES = 8
BF16 = jnp.bfloat16
F32 = jnp.float32
VMEM_SPEC = pl.BlockSpec(memory_space=pltpu.VMEM)
SMEM_SPEC = pl.BlockSpec(memory_space=pltpu.SMEM)


def dot(a, b):
    return jnp.dot(a, b, preferred_element_type=F32)


def iota(shape, axis):
    return lax.broadcasted_iota(jnp.int32, shape, axis)


def spread_mpo(mpo_own, mpo_other, share, phys, phys_own):
    terms = mpo_own.shape[1]
    rows = terms * phys * phys_own
    depth = 2 * share * LANE_ROWS
    pairs = phys * phys

    def kernel(own_ref, other_ref, out_ref):
        core = lax.axis_index("gz")
        shape = (rows, terms)
        spread = iota(shape, 0) // (phys * phys_own) == iota(shape, 1)
        spread = spread.astype(F32).astype(BF16)
        shape = (rows, share * pairs)
        row, column = iota(shape, 0), iota(shape, 1) % pairs
        wanted = (core * phys_own + row % phys_own) * phys + row // phys_own % phys
        wide = None
        for side, ref in enumerate((own_ref, other_ref)):
            chosen = lax.dot_general(
                spread, ref[...], (((1,), (1,)), ((), ())), preferred_element_type=F32
            )
            chosen = jnp.where(column == wanted, chosen, 0.0).astype(BF16)
            shape = (share * pairs, depth)
            widen = iota(shape, 0) // pairs + side * share == iota(shape, 1) // LANE_ROWS
            part = dot(chosen, widen.astype(F32).astype(BF16))
            wide = part if wide is None else wide + part
        shape = (LANE_ROWS, depth)
        same = (iota(shape, 0) == iota(shape, 1) % LANE_ROWS).astype(F32)
        tall = wide[:, None, :] * same[None, :, :]
        out_ref[...] = tall.reshape(rows * LANE_ROWS, depth).astype(BF16)

    return pl.pallas_call(
        kernel,
        out_shape=jax.ShapeDtypeStruct((rows * LANE_ROWS, depth), BF16),
        in_specs=[VMEM_SPEC] * 2,
        out_specs=VMEM_SPEC,
        compiler_params=pltpu.CompilerParams(vmem_limit_bytes=8 << 20),
        cost_estimate=pl.CostEstimate(
            flops=1 << 28, bytes_accessed=2 * rows * LANE_ROWS * depth, transcendentals=0
        ),
        name="spread_mpo",
    )(mpo_own, mpo_other)


def mix_right(lhs, right_own, right_other, terms, phys, phys_own):
    rows, cols = right_own.shape[1:]
    lhs_rows, depth = lhs.shape
    groups = terms * phys
    width = MIX_TILES * LANE_ROWS
    chunk = min(lhs_rows, MIX_ROWS)
    row_tiles = rows // LANE_ROWS

    def kernel(lhs_ref, own_ref, other_ref, out_ref):
        def tile(step, carry):
            parts = []
            for t in range(MIX_TILES):
                begin = pl.multiple_of(step * width + t * LANE_ROWS, LANE_ROWS)
                here = pl.ds(begin, LANE_ROWS)
                sides = [ref[:, here, :].reshape(-1, cols) for ref in (own_ref, other_ref)]
                parts.append(jnp.concatenate(sides, 0))
            rhs = jnp.concatenate(parts, 1)
            for start in range(0, lhs_rows, chunk):
                part = dot(lhs_ref[start : start + chunk, :], rhs).astype(BF16)
                part = part.reshape(chunk // LANE_ROWS, LANE_ROWS, MIX_TILES * cols)
                for i in range(chunk // LANE_ROWS):
                    group, p = divmod(start // LANE_ROWS + i, phys_own)
                    for t in range(MIX_TILES):
                        out_ref[group, step * MIX_TILES + t, :, p * cols : (p + 1) * cols] = part[
                            i, :, t * cols : (t + 1) * cols
                        ]
            return carry

        lax.fori_loop(0, rows // width, tile, 0)

    out = pl.pallas_call(
        kernel,
        out_shape=jax.ShapeDtypeStruct((groups, row_tiles, LANE_ROWS, phys_own * cols), BF16),
        in_specs=[VMEM_SPEC] * 3,
        out_specs=VMEM_SPEC,
        compiler_params=pltpu.CompilerParams(vmem_limit_bytes=20 << 20),
        cost_estimate=pl.CostEstimate(
            flops=2 * lhs_rows * depth * cols * row_tiles,
            bytes_accessed=2 * groups * rows * phys_own * cols,
            transcendentals=0,
        ),
        name="mix_right",
    )(lhs, right_own, right_other)
    return out.reshape(terms, phys * rows, phys_own * cols)


def apply_blocks(
    hops, sides, partner, blocks, total, left, mixed, charges, order, dims=None
):
    terms, rows, depth = left.shape
    out_cols = mixed.shape[2]
    half, _, cols = blocks[0][0].shape
    held = half * len(sides)
    first, last = total is None, dims is not None

    def kernel(charges_ref, order_ref, *refs):
        refs = list(refs)
        dims_ref = refs.pop(0) if last else None
        total_ref = None if first else refs.pop(0)
        left_ref, mixed_ref = refs[:2]
        block_refs = refs[2 : 2 + len(hops) * len(sides)]
        out_ref, term_list, block_list, sources = refs[2 + len(block_refs) :][:4]
        acc = refs[-1] if last else out_ref
        me, core = lax.axis_index("gx"), lax.axis_index("gz")
        whole = len(sides) == 2
        begin = 0 if whole else (1 - core if sides[0] else core) * half * cols
        begin = begin if whole else pl.multiple_of(begin, half * cols)
        count = jnp.int32(0)
        for i, hop in enumerate(hops):
            shift = order_ref[partner(me, hop)] - order_ref[me] + 1
            for u in range(terms):
                term_list[count] = u
                block_list[count] = i
                count += (charges_ref[u] == shift).astype(jnp.int32)
            for k, side in enumerate(sides):
                which = (1 - core if side else core) if whole else 0
                for q in range(half):
                    sources[i, which * half + q] = block_refs[i * len(sides) + k][q]
        acc[...] = jnp.zeros_like(acc) if first else total_ref[...]

        def add(start, many):
            sums = None
            for k in range(many):
                u, i = term_list[start + k], block_list[start + k]
                env = left_ref[u]
                applied = [dot(env, sources[i, q]).astype(BF16) for q in range(held)]
                weights = mixed_ref[u, pl.ds(begin, held * cols), :]
                piece = dot(jnp.concatenate(applied, 1), weights)
                sums = piece if sums is None else sums + piece
            acc[...] += sums

        def four(i, carry):
            add(4 * i, 4)
            return carry

        lax.fori_loop(0, count // 4, four, 0)
        rest = count % 4

        @pl.when(rest >= 2)
        def _():
            add(count - rest, 2)

        @pl.when(rest % 2 == 1)
        def _():
            add(count - 1, 1)

        if last:
            keep = iota((rows, out_cols), 0) < dims_ref[me]
            masked = jnp.where(keep, acc[...], 0.0)
            out_ref[...] = masked.reshape(rows, out_cols // cols, cols).astype(BF16)

    slots = terms * len(hops) + 1
    scratch = [
        pltpu.SMEM((slots,), jnp.int32),
        pltpu.SMEM((slots,), jnp.int32),
        pltpu.VMEM((len(hops), held, depth, cols), BF16),
    ]
    if last:
        scratch.append(pltpu.VMEM((rows, out_cols), F32))
        out_shape = jax.ShapeDtypeStruct((rows, out_cols // cols, cols), BF16)
    else:
        out_shape = jax.ShapeDtypeStruct((rows, out_cols), F32)
    scalars = [charges, order] + ([dims] if last else [])
    arrays = ([] if first else [total]) + [left, mixed]
    arrays += [block for parts in blocks for block in parts]
    block_bytes = 2 * depth * held * cols
    return pl.pallas_call(
        kernel,
        out_shape=out_shape,
        in_specs=[SMEM_SPEC] * len(scalars) + [VMEM_SPEC] * len(arrays),
        out_specs=VMEM_SPEC,
        scratch_shapes=scratch,
        compiler_params=pltpu.CompilerParams(
            vmem_limit_bytes=(8 << 20) + 2 * len(hops) * block_bytes
        ),
        cost_estimate=pl.CostEstimate(
            flops=2 * (terms // 3) * rows * held * cols * len(hops) * (depth + out_cols),
            bytes_accessed=2 * rows * out_cols * 4,
            transcendentals=0,
        ),
        name="apply_blocks",
    )(*scalars, *arrays)


def gather_blocks(own, axis):
    count = lax.axis_size(axis)
    blocks = {0: own}
    if count & (count - 1):
        steps = [(0, hop, [(i, (i + hop) % count) for i in range(count)]) for hop in range(1, count)]
        partner = lambda me, hop: lax.rem(me - hop + count, count)
    else:
        steps = []
        bit = count // 2
        while bit:
            pairs = [(i, i ^ bit) for i in range(count)]
            held = [0] + [hop for _, hop, _ in steps]
            steps += [(hop, hop | bit, pairs) for hop in held]
            bit //= 2
        partner = lambda me, hop: lax.bitwise_xor(me, hop)
    for source, hop, pairs in steps:
        blocks[hop] = lax.ppermute(blocks[source], axis, pairs)
    return blocks, partner


def use_stages(count):
    order = sorted(range(1, count), key=lambda hop: (bin(hop).count("1"), -hop))
    stages = [([0], (0, 1)), (order[:-1], (0, 1)), (order[-1:], (0,)), (order[-1:], (1,))]
    return [stage for stage in stages if stage[0]]


def step(state, left_env, mpo_terms, right_env, term_charge, charge_order, sector_dims):
    terms, share, phys, _ = mpo_terms.shape
    cores = lax.axis_size("gz")
    assert state.shape[0] == 1 and cores == 2
    half = phys // cores
    core = lax.axis_index("gz")
    swap = [(0, 1), (1, 0)]
    planes = state[0].transpose(1, 0, 2)
    own = lax.dynamic_slice_in_dim(planes, core * half, half, 0)
    own_other = lax.dynamic_slice_in_dim(planes, (1 - core) * half, half, 0)
    own, own_other, right_sent = lax.optimization_barrier((own, own_other, right_env))
    blocks, partner = gather_blocks(own, "gx")
    right_other = lax.ppermute(right_sent, "gz", swap)
    mpo_rows = mpo_terms.transpose(1, 2, 3, 0).reshape(share * phys * phys, terms)
    mpo_other = lax.ppermute(mpo_rows, "gz", swap)
    lhs = spread_mpo(mpo_rows, mpo_other, share, phys, half)
    mixed = mix_right(lhs, right_env, right_other, terms, phys, half)
    left = left_env[:, 0]

    halves = {0: (own, own_other)}
    for hop, block in blocks.items():
        if hop:
            halves[hop] = (block, lax.ppermute(block, "gz", swap))
    total = None
    stages = use_stages(lax.axis_size("gx"))
    for number, (hops, sides) in enumerate(stages):
        dims = sector_dims if number == len(stages) - 1 else None
        parts = [[halves[hop][side] for side in sides] for hop in hops]
        total = apply_blocks(
            hops, sides, partner, parts, total, left, mixed, term_charge, charge_order, dims
        )
    return total[None]


def solution(mesh):
    return jax.shard_map(
        step,
        mesh=mesh,
        in_specs=(
            P(("ga", "gx"), None, None, "gy"),
            P(None, ("ga", "gx"), None, None),
            P(None, "gz", None, None),
            P("gz", ("ga", "gy"), None),
            P(),
            P("ga"),
            P("ga"),
        ),
        out_specs=P(("ga", "gx"), None, "gz", "gy"),
        check_vma=False,
    )
```

time: 44.9 us -> 44.2 us (0.984)
  other arithmetic: 0.81 us -> 0 us
  local copies, waits for them, and re-layouts: 4.7 us -> 3.96 us
  Pallas kernels: 15.6 us -> 16.3 us
    another operation x3 -> x1, local copies, waits for them, and re-layouts: 3.31 us -> 1.89 us
    pallas_call x2 -> x4, Pallas kernels: 10.3 us -> 11.1 us  [apply_blocks(): pl.pallas_call(kernel, out_shape=out_shape, in_specs=[SMEM_SPEC] * len(sc...]
    transpose x1 -> x0, other arithmetic: 0.81 us -> none  [step(): mpo_all.transpose(0, 3, 2, 1).reshape(terms * phys * phys, cores * share)]
    unnamed x12, local copies, waits for them, and re-layouts: 1.24 us -> 2 us
    pallas_call x1, Pallas kernels: 5.29 us -> 4.71 us  [mix_right(): pl.pallas_call(kernel, out_shape=jax.ShapeDtypeStruct((groups, row_tiles,...]
    pallas_call x0 -> x1, Pallas kernels: none -> 0.51 us  [spread_mpo(): pl.pallas_call(kernel, out_shape=jax.ShapeDtypeStruct((rows * LANE_ROWS,...]
  transfers between devices with their start and end apart: 8 -> 8, of which waited for: 3 -> 3; matrix products, arithmetic and copies ran while one was open for 10% -> 0% of each run, Pallas kernels for 31% -> 33%
where the time goes in v2:
time: 44.2 us; the launch traced here: 44 us
  waiting for transfers between devices  16.6 us (38%)
  Pallas kernels  16.3 us (37%)
  starting transfers between devices  7.02 us (16%)
  local copies, waits for them, and re-layouts  3.96 us (9%)
    ppermute x3, waiting for transfers between devices, gather_blocks(): blocks[hop] = lax.ppermute(blocks[source], axis, pairs)  15.1 us
    pallas_call x4, Pallas kernels, apply_blocks(): pl.pallas_call(kernel, out_shape=out_shape, in_specs=[SMEM_SPEC] * len(sc...  11.1 us
    ppermute x3, starting transfers between devices, gather_blocks(): blocks[hop] = lax.ppermute(blocks[source], axis, pairs)  5.87 us
    pallas_call x1, Pallas kernels, mix_right(): pl.pallas_call(kernel, out_shape=jax.ShapeDtypeStruct((groups, row_tiles,...  4.71 us
    unnamed x12, local copies, waits for them, and re-layouts  2 us
    another operation x1, local copies, waits for them, and re-layouts  1.89 us
    ppermute x1, waiting for transfers between devices, step(): mpo_other = lax.ppermute(mpo_rows, 'gz', swap)  1.42 us
  transfers between devices with their start and end apart: 8, of which 3 were waited for; matrix products, arithmetic and copies ran while one was open for 0% of the time, Pallas kernels for 33%

profile of v2, /device:TPU:0, one launch (start us, length us, event | category | flops | bytes accessed | tf_op | source)
XLA Modules:
  0.0 44.0 jit_solution(10823441568628133184)
XLA Ops:
  0.0 1.9 %constant_dynamic-slice_fusion = (bf16[1,256,2,256]{3,2,1,0:T(2,128)(2,1)S(1)}, bf16[1,256,2,256]{3,2,1,0:T(2,128)(2,1)S(1)}) fusion(bf16[1,256,4,256]{3,2,1,0:T(4,128)(2,1)} %param.7, s32[]{:T(128)S(6)} %select_n.7, s32[]{:T(128)S(6)} %select_n.6), kind=kLoop, calls=%fused_computation.2 | loop fusion | bytes 1048584 | tf_op jit(solution)/shard_map/dynamic-slice.3
  1.9 0.1 copy_bitcast_fusion
  2.0 0.6 %collective-permute-start.1 = (bf16[8,256,256]{2,1,0:T(8,128)(2,1)}, bf16[8,256,256]{2,1,0:T(8,128)(2,1)S(1)}, u32[]{:S(2)}, u32[]{:S(2)}) collective-permute-start(bf16[8,256,256]{2,1,0:T(8,128)(2,1)} %own_ref.1), channel_id=1, source_target_pairs={{0,1},{1,0},{2,3},{3,2},{4,5},{5,4},{6,7},{7,6},{8,9},{9,8},{10,11... | collective-permute-start | bytes 3145736 | tf_op jit(solution)/shard_map/ppermute | solution.py:250
  2.6 3.7 %collective-permute-start.2 = (bf16[2,256,256]{2,1,0:T(8,128)(2,1)S(1)}, bf16[2,256,256]{2,1,0:T(8,128)(2,1)S(1)}, u32[]{:S(2)}, u32[]{:S(2)}) collective-permute-start(bf16[2,256,256]{2,1,0:T(8,128)(2,1)S(1)} %get-tuple-element.9.refs_2_), channel_id=1, source_target_pairs={{0,8},{4,12},{8,0},{12,4},{1,9},{5,13},{9,1},{13,5},{2,10},{6,14},... | collective-permute-start | bytes 786440 | tf_op jit(solution)/shard_map/ppermute | solution.py:228
  6.2 1.6 %collective-permute-start.4 = (bf16[2,256,256]{2,1,0:T(8,128)(2,1)S(1)}, bf16[2,256,256]{2,1,0:T(8,128)(2,1)S(1)}, u32[]{:S(2)}, u32[]{:S(2)}) collective-permute-start(bf16[2,256,256]{2,1,0:T(8,128)(2,1)S(1)} %get-tuple-element.9.refs_2_), channel_id=1, source_target_pairs={{0,4},{4,0},{8,12},{12,8},{1,5},{5,1},{9,13},{13,9},{2,6},{6,2},{1... | collective-permute-start | bytes 786440 | tf_op jit(solution)/shard_map/ppermute | solution.py:228
  7.8 11.0 %collective-permute-done.2.refs_3_ = bf16[2,256,256]{2,1,0:T(8,128)(2,1)S(1)} collective-permute-done((bf16[2,256,256]{2,1,0:T(8,128)(2,1)S(1)}, bf16[2,256,256]{2,1,0:T(8,128)(2,1)S(1)}, u32[]{:S(2)}, u32[]{:S(2)}) %collective-permute-start.2) | collective-permute-done | bytes 262176 | tf_op jit(solution)/shard_map/ppermute | solution.py:228
  18.8 0.6 %collective-permute-start.6 = (bf16[2,256,256]{2,1,0:T(8,128)(2,1)S(1)}, bf16[2,256,256]{2,1,0:T(8,128)(2,1)S(1)}, u32[]{:S(2)}, u32[]{:S(2)}) collective-permute-start(bf16[2,256,256]{2,1,0:T(8,128)(2,1)S(1)} %collective-permute-done.2.refs_3_), channel_id=1, source_target_pairs={{0,4},{4,0},{8,12},{12,8},{1,5},{5,1},{9,13},{13,9},{2,6},{6,2},{1... | collective-permute-start | bytes 786440 | tf_op jit(solution)/shard_map/ppermute | solution.py:228
  19.5 0.0 collective-permute-start
  19.5 1.4 %collective-permute-done.other_ref = bf16[128,16]{1,0:T(8,128)(2,1)S(1)} collective-permute-done((bf16[128,16]{1,0:T(8,128)(2,1)}, bf16[128,16]{1,0:T(8,128)(2,1)S(1)}, u32[]{:S(2)}, u32[]{:S(2)}) %collective-permute-start) | collective-permute-done | bytes 4128 | tf_op jit(solution)/shard_map/ppermute | solution.py:252
  20.9 0.8 %copy-done.2 = bf16[16,8,4,4]{0,3,2,1:T(4,128)(2,1)S(1)} copy-done((bf16[16,8,4,4]{0,3,2,1:T(4,128)(2,1)S(1)}, bf16[16,8,4,4]{0,3,2,1:T(4,128)(2,1)}, u32[]{:S(2)}) %copy-start.2) | copy-done | bytes 4120
  21.6 0.5 %spread_mpo.1.lhs_ref = bf16[2048,256]{1,0:T(8,128)(2,1)S(1)} custom-call(bf16[128,16]{1,0:T(8,128)(2,1)S(1)} %bitcast.23, bf16[128,16]{1,0:T(8,128)(2,1)S(1)} %collective-permute-done.other_ref), custom_call_target="tpu_custom_call" | custom-call | flops 268435456 | bytes 1048576 | tf_op jit(solution)/shard_map/spread_mpo/pallas_call | solution.py:55
  22.2 0.2 collective-permute-start.3
  22.4 0.0 collective-permute-done.4.refs_5_
  22.4 0.3 collective-permute-start.5
  22.7 4.1 %collective-permute-done.6.refs_3_ = bf16[2,256,256]{2,1,0:T(8,128)(2,1)S(1)} collective-permute-done((bf16[2,256,256]{2,1,0:T(8,128)(2,1)S(1)}, bf16[2,256,256]{2,1,0:T(8,128)(2,1)S(1)}, u32[]{:S(2)}, u32[]{:S(2)}) %collective-permute-start.6) | collective-permute-done | bytes 262176 | tf_op jit(solution)/shard_map/ppermute | solution.py:228
  26.8 0.0 collective-permute-start.7
  26.8 1.2 %copy-done.1 = bf16[8,256,256]{2,1,0:T(8,128)(2,1)S(1)} copy-done((bf16[8,256,256]{2,1,0:T(8,128)(2,1)S(1)}, bf16[8,256,256]{2,1,0:T(8,128)(2,1)}, u32[]{:S(2)}) %copy-start.1) | copy-done | bytes 1048600
  28.1 4.7 %mix_right.1 = bf16[64,16,16,512]{3,2,1,0:T(8,128)(2,1)S(1)} custom-call(bf16[2048,256]{1,0:T(8,128)(2,1)S(1)} %spread_mpo.1.lhs_ref, bf16[8,256,256]{2,1,0:T(8,128)(2,1)S(1)} %copy-done.1, bf16[8,256,256]{2,1,0:T(8,128)(2,1)S(1)} %collective-permute-done.1.other_ref), custom_call_target="tpu_custom_call" | custom-call | flops 4294967296 | bytes 16777216 | tf_op jit(solution)/shard_map/mix_right/pallas_call | solution.py:98
  32.8 3.0 %apply_blocks.4.refs_0_ = f32[256,512]{1,0:T(8,128)S(1)} custom-call(s32[16]{0:T(128)S(1)} %copy-done.3, s32[4]{0:T(128)S(1)} %copy-done.4, bf16[16,256,256]{2,1,0:T(8,128)(2,1)S(1)} %bitcast.18, bf16[16,1024,512]{2,1,0:T(8,128)(2,1)S(1)} %bitcast.14, bf16[2,256,256]{2,1,0:T(8,128)(2,1)S(1)} %get-tuple-element.9.refs_2_, ...), custom_call_target="tpu_custom_call" | custom-call | flops 2013265920 | bytes 1048576 | tf_op jit(solution)/shard_map/apply_blocks/pallas_call | solution.py:194
  35.8 0.0 copy-start.5
  35.8 0.0 collective-permute-done.3.refs_4_
  35.9 5.9 %apply_blocks.5.refs_0_ = f32[256,512]{1,0:T(8,128)S(1)} custom-call(s32[16]{0:T(128)S(1)} %copy-done.3, s32[4]{0:T(128)S(1)} %copy-done.4, f32[256,512]{1,0:T(8,128)S(1)} %apply_blocks.4.refs_0_, bf16[16,256,256]{2,1,0:T(8,128)(2,1)S(1)} %bitcast.19, bf16[16,1024,512]{2,1,0:T(8,128)(2,1)S(1)} %bitcast.15, ...), custom_call_target="tpu_custom_call" | custom-call | flops 4026531840 | bytes 1048576 | tf_op jit(solution)/shard_map/apply_blocks/pallas_call | solution.py:194
  41.7 0.6 %apply_blocks.6.refs_1_ = f32[256,512]{1,0:T(8,128)S(1)} custom-call(s32[16]{0:T(128)S(1)} %copy-done.3, s32[4]{0:T(128)S(1)} %copy-done.4, f32[256,512]{1,0:T(8,128)S(1)} %apply_blocks.5.refs_0_, bf16[16,256,256]{2,1,0:T(8,128)(2,1)S(1)} %bitcast.20, bf16[16,1024,512]{2,1,0:T(8,128)(2,1)S(1)} %bitcast.16, ...), custom_call_target="tpu_custom_call" | custom-call | flops 1006632960 | bytes 1048576 | tf_op jit(solution)/shard_map/apply_blocks/pallas_call | solution.py:194
  42.4 1.6 %apply_blocks.7 = bf16[256,2,256]{2,1,0:T(2,128)(2,1)} custom-call(s32[16]{0:T(128)S(1)} %copy-done.3, s32[4]{0:T(128)S(1)} %copy-done.4, s32[4]{0:T(128)S(1)} %copy-done.5, f32[256,512]{1,0:T(8,128)S(1)} %apply_blocks.6.refs_1_, bf16[16,256,256]{2,1,0:T(8,128)(2,1)S(1)} %bitcast.21, bf16[16,1024,512]{2,1,0:T(8,128)(2,1)S(1)} %bitcast.17, ...), custom_call_target="tpu_custom_call" | custom-call | flops 1006632960 | bytes 1048576 | tf_op jit(solution)/shard_map/apply_blocks/pallas_call | solution.py:194
  (12 shorter events, 0.0 us)
Async XLA Ops:
  0.0 32.8 %copy-start = (bf16[16,1,256,256]{3,2,1,0:T(8,128)(2,1)S(1)}, bf16[16,1,256,256]{3,2,1,0:T(8,128)(2,1)}, u32[]{:S(2)}) copy-start(bf16[16,1,256,256]{3,2,1,0:T(8,128)(2,1)} %param.8) | copy-start | bytes 6291460
  0.0 32.8 %copy-start.3 = (s32[16]{0:T(128)S(1)}, s32[16]{0:T(128)}, u32[]{:S(2)}) copy-start(s32[16]{0:T(128)} %charges_ref.7) | copy-start | bytes 196
  0.0 32.8 %copy-start.4 = (s32[4]{0:T(128)S(1)}, s32[4]{0:T(128)}, u32[]{:S(2)}) copy-start(s32[4]{0:T(128)} %order_ref.7) | copy-start | bytes 52
  2.0 24.9 %collective-permute-start.1 = (bf16[8,256,256]{2,1,0:T(8,128)(2,1)}, bf16[8,256,256]{2,1,0:T(8,128)(2,1)S(1)}, u32[]{:S(2)}, u32[]{:S(2)}) collective-permute-start(bf16[8,256,256]{2,1,0:T(8,128)(2,1)} %own_ref.1), channel_id=1, source_target_pairs={{0,1},{1,0},{2,3},{3,2},{4,5},{5,4},{6,7},{7,6},{8,9},{9,8},{10,11... | collective-permute-start | bytes 3145736 | tf_op jit(solution)/shard_map/ppermute | solution.py:250
  2.6 16.3 %collective-permute-start.2 = (bf16[2,256,256]{2,1,0:T(8,128)(2,1)S(1)}, bf16[2,256,256]{2,1,0:T(8,128)(2,1)S(1)}, u32[]{:S(2)}, u32[]{:S(2)}) collective-permute-start(bf16[2,256,256]{2,1,0:T(8,128)(2,1)S(1)} %get-tuple-element.9.refs_2_), channel_id=1, source_target_pairs={{0,8},{4,12},{8,0},{12,4},{1,9},{5,13},{9,1},{13,5},{2,10},{6,14},... | collective-permute-start | bytes 786440 | tf_op jit(solution)/shard_map/ppermute | solution.py:228
  6.2 16.2 %collective-permute-start.4 = (bf16[2,256,256]{2,1,0:T(8,128)(2,1)S(1)}, bf16[2,256,256]{2,1,0:T(8,128)(2,1)S(1)}, u32[]{:S(2)}, u32[]{:S(2)}) collective-permute-start(bf16[2,256,256]{2,1,0:T(8,128)(2,1)S(1)} %get-tuple-element.9.refs_2_), channel_id=1, source_target_pairs={{0,4},{4,0},{8,12},{12,8},{1,5},{5,1},{9,13},{13,9},{2,6},{6,2},{1... | collective-permute-start | bytes 786440 | tf_op jit(solution)/shard_map/ppermute | solution.py:228
  18.8 8.0 %collective-permute-start.6 = (bf16[2,256,256]{2,1,0:T(8,128)(2,1)S(1)}, bf16[2,256,256]{2,1,0:T(8,128)(2,1)S(1)}, u32[]{:S(2)}, u32[]{:S(2)}) collective-permute-start(bf16[2,256,256]{2,1,0:T(8,128)(2,1)S(1)} %collective-permute-done.2.refs_3_), channel_id=1, source_target_pairs={{0,4},{4,0},{8,12},{12,8},{1,5},{5,1},{9,13},{13,9},{2,6},{6,2},{1... | collective-permute-start | bytes 786440 | tf_op jit(solution)/shard_map/ppermute | solution.py:228
  19.5 1.4 %collective-permute-start = (bf16[128,16]{1,0:T(8,128)(2,1)}, bf16[128,16]{1,0:T(8,128)(2,1)S(1)}, u32[]{:S(2)}, u32[]{:S(2)}) collective-permute-start(bf16[128,16]{1,0:T(8,128)(2,1)} %bitcast.22), channel_id=1, source_target_pairs={{0,1},{1,0},{2,3},{3,2},{4,5},{5,4},{6,7},{7,6},{8,9},{9,8},{10,11... | collective-permute-start | bytes 12296 | tf_op jit(solution)/shard_map/ppermute | solution.py:252
  20.9 0.8 %copy-start.2 = (bf16[16,8,4,4]{0,3,2,1:T(4,128)(2,1)S(1)}, bf16[16,8,4,4]{0,3,2,1:T(4,128)(2,1)}, u32[]{:S(2)}) copy-start(bf16[16,8,4,4]{0,3,2,1:T(4,128)(2,1)} %param.9) | copy-start | bytes 12292
  22.2 13.7 %collective-permute-start.3 = (bf16[2,256,256]{2,1,0:T(8,128)(2,1)S(1)}, bf16[2,256,256]{2,1,0:T(8,128)(2,1)S(1)}, u32[]{:S(2)}, u32[]{:S(2)}) collective-permute-start(bf16[2,256,256]{2,1,0:T(8,128)(2,1)S(1)} %collective-permute-done.2.refs_3_), channel_id=1, source_target_pairs={{0,1},{1,0},{2,3},{3,2},{4,5},{5,4},{6,7},{7,6},{8,9},{9,8},{10,11... | collective-permute-start | bytes 786440 | tf_op jit(solution)/shard_map/ppermute | solution.py:260
  22.4 13.5 %collective-permute-start.5 = (bf16[2,256,256]{2,1,0:T(8,128)(2,1)S(1)}, bf16[2,256,256]{2,1,0:T(8,128)(2,1)S(1)}, u32[]{:S(2)}, u32[]{:S(2)}) collective-permute-start(bf16[2,256,256]{2,1,0:T(8,128)(2,1)S(1)} %collective-permute-done.4.refs_5_), channel_id=1, source_target_pairs={{0,1},{1,0},{2,3},{3,2},{4,5},{5,4},{6,7},{7,6},{8,9},{9,8},{10,11... | collective-permute-start | bytes 786440 | tf_op jit(solution)/shard_map/ppermute | solution.py:260
  26.8 15.5 %collective-permute-start.7 = (bf16[2,256,256]{2,1,0:T(8,128)(2,1)S(1)}, bf16[2,256,256]{2,1,0:T(8,128)(2,1)S(1)}, u32[]{:S(2)}, u32[]{:S(2)}) collective-permute-start(bf16[2,256,256]{2,1,0:T(8,128)(2,1)S(1)} %collective-permute-done.6.refs_3_), channel_id=1, source_target_pairs={{0,1},{1,0},{2,3},{3,2},{4,5},{5,4},{6,7},{7,6},{8,9},{9,8},{10,11... | collective-permute-start | bytes 786440 | tf_op jit(solution)/shard_map/ppermute | solution.py:260
  26.8 1.2 %copy-start.1 = (bf16[8,256,256]{2,1,0:T(8,128)(2,1)S(1)}, bf16[8,256,256]{2,1,0:T(8,128)(2,1)}, u32[]{:S(2)}) copy-start(bf16[8,256,256]{2,1,0:T(8,128)(2,1)} %own_ref.1) | copy-start | bytes 3145732
  35.8 6.6 %copy-start.5 = (s32[4]{0:T(128)S(1)}, s32[4]{0:T(128)}, u32[]{:S(2)}) copy-start(s32[4]{0:T(128)} %refs_0_.1) | copy-start | bytes 52
